TPU v7x, 32 devices: a whole 2x2x4 slice. The times are simulated.
32 devices in a mesh: seq: 8 (over y, x, core), cb: 4 (over z).
Axes of the slice: x: 2, y: 2, z: 4, core: 2. Of those that a mesh axis runs over, the one named last changes fastest.
Arguments:
- hidden: bfloat16 [2, 1024, 4096], P(None, 'seq'), may hold values from -6 to 6
- temporal_gain: float32 [4096], replicated, may hold values from 0.5 to 2
- temporal_qkv: bfloat16 [3, 4096, 2048], P(None, None, 'cb'), may hold values from -10 to 10
- temporal_out: bfloat16 [2048, 4096], P('cb'), may hold values from -0.125 to 0.125
- codebook_ids: int32 [2, 1024, 4], P(None, 'seq', 'cb'), may hold values from 0 to 2047
- embedding: bfloat16 [4, 2048, 1024], P('cb'), may hold values from -6 to 6
- input_weight: bfloat16 [4, 4096, 1024], P('cb', 'seq'), may hold values from -0.09375 to 0.09375
- depth_gain: float32 [4, 1024], P('cb'), may hold values from 0.5 to 2
- depth_qkv: bfloat16 [4, 3, 1024, 1024], P('cb'), may hold values from -10 to 10
- depth_out: bfloat16 [4, 1024, 1024], P('cb'), may hold values from -0.1875 to 0.1875
Outputs:
- temporal: bfloat16 [2, 1024, 4096], P(None, 'seq')
- depth: bfloat16 [2, 1024, 4, 1024], P(None, 'seq', 'cb')
All inputs are finite; a program needn't handle non-finite values.
Results may differ from a plain program's by a relative error of at most 0.017.
Values may be sent and summed in bfloat16 or wider, within the bound.
No kernel may reach another device: no remote copies, remote signals or barrier semaphores. Data moves between devices by JAX's collectives and lax.ppermute only.
A program may use at most 128 MiB of HBM per device.

v0:
```python
import jax
import jax.numpy as jnp
from jax import lax
from jax.sharding import PartitionSpec as P

HD = 128
DW = 1024
DH = 16
DHD = 64


def normalize(values, scale):
    mean_sq = jnp.mean(values * values, axis=-1, keepdims=True)
    return values * lax.rsqrt(mean_sq + 1e-05) * scale


def shards(
    hidden,
    temporal_gain,
    temporal_qkv,
    temporal_out,
    codebook_ids,
    embedding,
    input_weight,
    depth_gain,
    depth_qkv,
    depth_out,
):
    seq_count, frames, width = hidden.shape
    head_cols = temporal_qkv.shape[2]
    head_count = head_cols // HD
    row_count = seq_count * frames
    hidden_f = hidden.astype(jnp.float32)
    normed = normalize(hidden_f, temporal_gain).astype(jnp.bfloat16).reshape(row_count, width)
    projected = []
    for which in range(3):
        part_rows = jnp.dot(normed, temporal_qkv[which], preferred_element_type=jnp.float32).astype(
            jnp.bfloat16
        )
        projected.append(part_rows.reshape(seq_count, frames, head_count, HD))
    queries = projected[0]
    query_pos = lax.axis_index("seq") * frames + jnp.arange(frames, dtype=jnp.int32)
    temporal_scale = 1.0 / jnp.sqrt(jnp.float32(HD))
    highest = jnp.full((seq_count, head_count, frames), -1e30, jnp.float32)
    key_piece = lax.all_gather(projected[1], "seq", axis=1, tiled=True)
    value_piece = lax.all_gather(projected[2], "seq", axis=1, tiled=True)
    count = key_piece.shape[1]
    scores = (
        jnp.einsum("sqhd,skhd->shqk", queries, key_piece, preferred_element_type=jnp.float32)
        * temporal_scale
    )
    key_pos = jnp.arange(count, dtype=jnp.int32)
    allowed = (key_pos[None, :] <= query_pos[:, None])[None, None]
    scores = jnp.where(allowed, scores, -1e30)
    new_high = jnp.maximum(highest, jnp.max(scores, axis=-1))
    weights = jnp.where(allowed, jnp.exp(scores - new_high[..., None]), 0.0)
    totals = jnp.sum(weights, axis=-1)
    update = jnp.einsum(
        "shqk,skhd->sqhd",
        weights.astype(jnp.bfloat16),
        value_piece,
        preferred_element_type=jnp.float32,
    )
    gathered = update
    highest, totals, gathered = (new_high, totals, gathered)
    mixed = (
        (gathered / totals.transpose(0, 2, 1)[..., None])
        .astype(jnp.bfloat16)
        .reshape(row_count, head_cols)
    )
    term = jnp.dot(mixed, temporal_out, preferred_element_type=jnp.float32)
    summed = lax.psum(term.astype(jnp.bfloat16), "cb").astype(jnp.float32)
    temporal = (hidden_f.reshape(row_count, width) + summed).astype(jnp.bfloat16)
    projected_in = jnp.dot(
        temporal,
        lax.all_gather(input_weight, "seq", axis=1, tiled=True)[0],
        preferred_element_type=jnp.float32,
    )
    entry = jnp.take(embedding[0], codebook_ids.reshape(row_count), axis=0).astype(jnp.float32)
    stream = (projected_in + entry).astype(jnp.bfloat16)
    depth_normed = normalize(stream.astype(jnp.float32), depth_gain[0]).astype(jnp.bfloat16)
    book_query = jnp.dot(depth_normed, depth_qkv[0, 0], preferred_element_type=jnp.float32).astype(
        jnp.bfloat16
    )
    book_key = jnp.dot(depth_normed, depth_qkv[0, 1], preferred_element_type=jnp.float32).astype(
        jnp.bfloat16
    )
    book_value = jnp.dot(depth_normed, depth_qkv[0, 2], preferred_element_type=jnp.float32).astype(
        jnp.bfloat16
    )
    depth_scale = 1.0 / jnp.sqrt(jnp.float32(DHD))
    books = lax.axis_size("cb")
    block_rows = row_count // books
    packed = jnp.concatenate([book_query, book_key, book_value], axis=1).reshape(
        1, books, block_rows, 3 * DW
    )
    arrived = lax.all_to_all(packed, "cb", split_axis=1, concat_axis=0, tiled=True)
    item_count = arrived.shape[2]
    body_rows = arrived.reshape(books, item_count, 3, DH, DHD)
    query_part = body_rows[:, :, 0]
    key_part = body_rows[:, :, 1]
    value_part = body_rows[:, :, 2]
    scores = (
        jnp.einsum("crhd,jrhd->crhj", query_part, key_part, preferred_element_type=jnp.float32)
        * depth_scale
    )
    numbers = jnp.arange(books, dtype=jnp.int32)
    permitted = (numbers[None, :] <= numbers[:, None])[:, None, None, :]
    scores = jnp.where(permitted, scores, -1e30)
    highest_l = jnp.max(scores, axis=-1, keepdims=True)
    weights = jnp.where(permitted, jnp.exp(scores - highest_l), 0.0)
    totals_l = jnp.sum(weights, axis=-1)[..., None]
    result = (
        jnp.einsum(
            "crhj,jrhd->crhd",
            weights.astype(jnp.bfloat16),
            value_part,
            preferred_element_type=jnp.float32,
        )
        / totals_l
    )
    result = result.astype(jnp.bfloat16).reshape(books, 1, item_count, DW)
    returned = lax.all_to_all(result, "cb", split_axis=0, concat_axis=1, tiled=True)
    book_mixed = returned.reshape(row_count, DW)
    depth = (
        jnp.dot(book_mixed, depth_out[0], preferred_element_type=jnp.float32)
        + stream.astype(jnp.float32)
    ).astype(jnp.bfloat16)
    return (temporal.reshape(seq_count, frames, width), depth.reshape(seq_count, frames, 1, DW))


def solution(mesh):
    placed = (
        P(None, "seq", None),
        P(),
        P(None, None, "cb"),
        P("cb", None),
        P(None, "seq", "cb"),
        P("cb", None, None),
        P("cb", "seq", None),
        P("cb", None),
        P("cb", None, None, None),
        P("cb", None, None),
    )
    return jax.shard_map(
        shards,
        mesh=mesh,
        in_specs=placed,
        out_specs=(P(None, "seq", None), P(None, "seq", "cb", None)),
        check_vma=False,
    )
```

profile of v0, /device:TPU:0, one launch (start us, length us, event | category | flops | bytes accessed | tf_op | source)
XLA Modules:
  0.0 334.3 jit_solution(7204706713739142722)
XLA Ops:
  7.2 0.0 copy-start
  7.2 0.0 all-gather.6.cloned.1.call-start
  7.2 2.2 multiply_reduce_fusion
  9.5 2.3 multiply_convert_fusion
  11.8 0.0 copy-start.2
  11.8 1.3 copy-done.2
  13.1 3.5 %fusion.63 = bf16[256,512]{1,0:T(8,128)(2,1)S(1)} fusion(bf16[256,4096]{1,0:T(8,128)(2,1)S(1)} %bitcast.119, bf16[3,4096,512]{2,1,0:T(8,128)(2,1)} %param.12), kind=kOutput, calls=%fused_computation.54 | convolution fusion | flops 1073872896 | bytes 6553600 | tf_op jit(solution)/shard_map/dot_general | solution.py:37
  16.6 0.1 reshape.148
  16.7 0.8 copy.53
  17.5 0.0 all-gather.6.cloned.1.call-update
  17.5 0.0 all-gather.4.cloned.1.call-start
  17.5 4.1 %fusion.57 = bf16[256,512]{1,0:T(8,128)(2,1)S(1)} fusion(bf16[256,4096]{1,0:T(8,128)(2,1)} %bitcast.120, bf16[3,4096,512]{2,1,0:T(8,128)(2,1)} %param.12), kind=kOutput, calls=%fused_computation.52 | convolution fusion | flops 1073872896 | bytes 6553600 | tf_op jit(solution)/shard_map/dot_general | solution.py:37
  21.6 0.1 reshape.146
  21.7 0.9 copy.52
  22.5 0.0 all-gather.4.cloned.1.call-update
  22.6 0.0 all-reduce.2.cloned.1.call-start
  22.6 4.1 %fusion.60 = bf16[256,512]{1,0:T(8,128)(2,1)S(1)} fusion(bf16[256,4096]{1,0:T(8,128)(2,1)} %bitcast.121, bf16[3,4096,512]{2,1,0:T(8,128)(2,1)} %param.12), kind=kOutput, calls=%fused_computation.53 | convolution fusion | flops 1073872896 | bytes 6553600 | tf_op jit(solution)/shard_map/dot_general | solution.py:37
  26.7 0.1 reshape.147
  26.8 0.1 iota_compare_fusion
  26.9 21.2 %all-gather.6.cloned.1.call-done = bf16[2,1024,4,128]{3,1,2,0:T(8,128)(2,1)} async-done(((bf16[2,128,4,128]{3,1,2,0:T(8,128)(2,1)}), bf16[2,1024,4,128]{3,1,2,0:T(8,128)(2,1)}) %all-gather.6.cloned.1.call-update) | async-done | bytes 2097168 | tf_op jit(solution)/shard_map/all_gather | solution.py:45
  48.1 2.6 fusion.12
  50.8 0.0 copy-start.1
  50.8 1.9 copy-done.1
  52.7 1.3 fusion.13
  54.0 24.7 %all-gather.4.cloned.1.call-done = bf16[2,1024,4,128]{1,3,2,0:T(8,128)(2,1)} async-done(((bf16[2,128,4,128]{1,3,2,0:T(8,128)(2,1)}), bf16[2,1024,4,128]{1,3,2,0:T(8,128)(2,1)}) %all-gather.4.cloned.1.call-update) | async-done | bytes 2097168 | tf_op jit(solution)/shard_map/all_gather | solution.py:46
  78.7 4.2 %fusion.73 = bf16[2,128,4,128]{1,3,2,0:T(8,128)(2,1)S(1)} fusion(bf16[2,1024,4,128]{1,3,2,0:T(8,128)(2,1)} %all-gather.4.cloned.1.call-done, f32[2,4,128,1024]{3,2,1,0:T(8,128)} %copy-done.1, f32[2,4,128]{2,1,0:T(4,128)S(1)} %broadcast_maximum_fusion, pred[128,1024]{1,0:T(8,128)(4,1)S(1)} %iota_compare_fusion, f32[2,128,4]{1,2,0:T(4,128)S(1)} %bitcast.126), kind=kOutput, calls=%fused_computation.63 | convolution fusion | flops 273940480 | bytes 6692864 | tf_op jit(solution)/shard_map/shqk,skhd->sqhd/dot_general | solution.py:58
  82.9 0.2 copy.55
  83.1 0.0 copy-start.3
  83.2 4.8 %convolution_convert_fusion = bf16[256,4096]{1,0:T(8,128)(2,1)} fusion(bf16[512,4096]{1,0:T(8,128)(2,1)} %param.13, bf16[32,8,4,128]{3,2,1,0:T(4,128)(2,1)S(1)} %bitcast.124), kind=kOutput, calls=%fused_computation.3 | convolution fusion | flops 1074790400 | bytes 6553600 | tf_op jit(solution)/shard_map/dot_general | solution.py:71
  87.9 0.0 all-reduce.2.cloned.1.call-update
  87.9 0.2 all-gather.8.cloned.1.call-start
  88.2 0.3 all-gather.8.cloned.1.call-update
  88.5 0.0 copy-done.3
  88.6 4.3 %gather_fusion = bf16[256,1024]{1,0:T(8,128)(2,1)S(1)} fusion(bf16[2048,1024]{1,0:T(8,128)(2,1)} %bitcast.117, s32[1024]{0:T(1024)S(1)} %pad_clamp_fusion), kind=kCustom, calls=%fused_computation | custom fusion | bytes 1049600 | tf_op jit(solution)/shard_map/jit(_take)/gather | solution.py:79
  92.9 81.4 %all-reduce.2.cloned.1.call-done = bf16[256,4096]{1,0:T(8,128)(2,1)} async-done(((bf16[256,4096]{1,0:T(8,128)(2,1)}), bf16[256,4096]{1,0:T(8,128)(2,1)}) %all-reduce.2.cloned.1.call-update) | async-done | bytes 2097168 | tf_op jit(solution)/shard_map/psum | solution.py:72
  174.2 4.3 %fusion.8 = bf16[256,4096]{1,0:T(8,128)(2,1)} fusion(bf16[256,4096]{1,0:T(8,128)(2,1)} %all-reduce.2.cloned.1.call-done, bf16[2,128,4096]{2,1,0:T(8,128)(2,1)} %param.10), kind=kLoop, calls=%fused_computation.11 | loop fusion | flops 4194304 | bytes 6291456 | tf_op jit(solution)/shard_map/convert_element_type | solution.py:73
  178.6 0.0 copy-start.4
  178.6 50.7 %all-gather.8.cloned.1.call-done = bf16[1,4096,1024]{2,1,0:T(8,128)(2,1)} async-done(((bf16[1,512,1024]{2,1,0:T(8,128)(2,1)}), bf16[1,4096,1024]{2,1,0:T(8,128)(2,1)}) %all-gather.8.cloned.1.call-update) | async-done | bytes 8388624 | tf_op jit(solution)/shard_map/all_gather | solution.py:76
  229.3 6.5 %fusion.66 = (f32[256]{0:T(256)S(1)}, bf16[256,1024]{1,0:T(8,128)(2,1)S(1)}) fusion(bf16[256,1024]{1,0:T(8,128)(2,1)S(1)} %gather_fusion, pred[256]{0:T(512)(128)(4,1)S(1)} %compare_and_fusion, bf16[256,4096]{1,0:T(8,128)(2,1)} %fusion.8, bf16[1,4096,1024]{2,1,0:T(8,128)(2,1)} %all-gather.8.cloned.1.call-done), kind=kOutput, calls=%fused_computation.55 | convolution fusion | flops 2149318400 | bytes 11535616 | tf_op jit(solution)/shard_map/dot_general | solution.py:74
  235.8 0.0 copy-start.5
  235.8 0.0 copy-done.4
  235.8 2.5 fusion.45
  238.3 2.4 fusion.48
  240.7 0.0 copy-done.5
  240.7 2.4 fusion.51
  243.1 1.3 pad_maximum_fusion
  244.3 4.6 %all-to-all-start = ((bf16[1,4,64,3072]{3,2,0,1:T(8,128)(2,1)}), bf16[1,4,64,3072]{3,2,0,1:T(8,128)(2,1)}, u32[]{:S(2)}, u32[]{:S(2)}) async-start(bf16[1,4,64,3072]{3,2,0,1:T(8,128)(2,1)} %bitcast.116), calls=%async_computation | async-start | bytes 3145728 | tf_op jit(solution)/shard_map/all_to_all | solution.py:97
  248.9 37.5 %all-to-all-done = bf16[1,4,64,3072]{3,2,0,1:T(8,128)(2,1)} async-done(((bf16[1,4,64,3072]{3,2,0,1:T(8,128)(2,1)}), bf16[1,4,64,3072]{3,2,0,1:T(8,128)(2,1)}, u32[]{:S(2)}, u32[]{:S(2)}) %all-to-all-start) | async-done | bytes 1572896 | tf_op jit(solution)/shard_map/all_to_all | solution.py:97
  286.4 4.9 %reshape.154 = bf16[4,64,3,16,64]{4,3,2,1,0:T(8,128)(2,1)} reshape(bf16[1,4,64,3072]{3,2,0,1:T(8,128)(2,1)} %all-to-all-done) | data formatting | bytes 3145728 | tf_op jit(solution)/shard_map/reshape | solution.py:99
  291.3 3.5 %fusion.89 = (bf16[4,64,1,16,64]{4,3,2,1,0:T(8,128)(2,1)}, bf16[4,64,1,16,64]{4,3,2,1,0:T(8,128)(2,1)S(1)}, bf16[4,64,1,16,64]{4,3,2,1,0:T(8,128)(2,1)S(1)}) fusion(bf16[4,64,3,16,64]{4,3,2,1,0:T(8,128)(2,1)} %reshape.154), kind=kLoop, calls=%fused_computation.86 | loop fusion | bytes 3145728 | tf_op jit(solution)/shard_map/slice | solution.py:102
  294.8 2.9 fusion.69
  297.7 2.4 copy.60
  300.1 0.1 fusion.80
  300.1 0.1 fusion.81
  300.3 1.8 copy.61
  302.1 1.1 copy.62
  303.2 2.9 fusion.32
  306.0 0.1 copy.63
  306.2 1.5 reshape.155
  307.7 17.5 %all_to_all.8 = bf16[4,1,64,1024]{3,2,1,0:T(8,128)(2,1)S(1)} all-to-all(bf16[4,1,64,1024]{3,2,1,0:T(8,128)(2,1)} %bitcast.122), channel_id=1, replica_groups=mesh['seq'=8,'cb'=4] {'cb'}, dimensions={0} | all-to-all | bytes 1048576 | tf_op jit(solution)/shard_map/all_to_all | solution.py:123
  325.2 0.0 copy-done
  325.2 2.5 fusion.42
  (8 shorter events, 0.0 us)
Async XLA Ops:
  7.2 318.0 %copy-start = (bf16[1,1024,1024]{2,1,0:T(8,128)(2,1)S(1)}, bf16[1,1024,1024]{2,1,0:T(8,128)(2,1)}, u32[]{:S(2)}) copy-start(bf16[1,1024,1024]{2,1,0:T(8,128)(2,1)} %param.19) | copy-start | bytes 6291460
  7.2 41.0 %all-gather.6.cloned.1.call-start = ((), (), s32[]{:S(2)}) async-start(), calls=%async_computation.3 | async-start | bytes 2359296 | tf_op jit(solution)/shard_map/all_gather | solution.py:45
  11.8 1.3 copy-start.2
  17.5 61.2 %all-gather.4.cloned.1.call-start = ((), (), s32[]{:S(2)}) async-start(), calls=%async_computation.2 | async-start | bytes 2359296 | tf_op jit(solution)/shard_map/all_gather | solution.py:46
  22.6 151.7 %all-reduce.2.cloned.1.call-start = ((), (), s32[]{:S(2)}) async-start(), calls=%async_computation.4 | async-start | bytes 4194304 | tf_op jit(solution)/shard_map/psum | solution.py:72
  50.8 1.9 copy-start.1
  83.1 5.4 %copy-start.3 = (s32[2,128,1]{1,2,0:T(1,128)S(1)}, s32[2,128,1]{1,2,0:T(1,128)}, u32[]{:S(2)}) copy-start(s32[2,128,1]{1,2,0:T(1,128)} %param.14) | copy-start | bytes 3076
  87.9 141.4 %all-gather.8.cloned.1.call-start = ((), (), s32[]{:S(2)}) async-start(), calls=%async_computation.5 | async-start | bytes 9437184 | tf_op jit(solution)/shard_map/all_gather | solution.py:76
  178.6 57.2 %copy-start.4 = (f32[1,1024]{1,0:T(1,128)S(1)}, f32[1,1024]{1,0:T(1,128)}, u32[]{:S(2)}) copy-start(f32[1,1024]{1,0:T(1,128)} %param.17) | copy-start | bytes 12292
  235.8 4.9 %copy-start.5 = (bf16[256,1024]{1,0:T(8,128)(2,1)}, bf16[256,1024]{1,0:T(8,128)(2,1)S(1)}, u32[]{:S(2)}) copy-start(bf16[256,1024]{1,0:T(8,128)(2,1)S(1)} %get-tuple-element.20) | copy-start | bytes 1572868
  244.3 42.1 %all-to-all-start = ((bf16[1,4,64,3072]{3,2,0,1:T(8,128)(2,1)}), bf16[1,4,64,3072]{3,2,0,1:T(8,128)(2,1)}, u32[]{:S(2)}, u32[]{:S(2)}) async-start(bf16[1,4,64,3072]{3,2,0,1:T(8,128)(2,1)} %bitcast.116), calls=%async_computation | async-start | bytes 3145728 | tf_op jit(solution)/shard_map/all_to_all | solution.py:97
Sparse Core Ops, SparseCore 0:
  17.6 30.4 all-gather.5
  50.6 28.0 all-gather.3
  88.1 86.1 all-reduce.1
  176.0 53.2 all-gather.7
where the time goes:
time: 335 us; the launch traced here: 334 us
  waiting for transfers between devices  216 us (64%)
  matrix products  45.2 us (13%)
  local copies, waits for them, and re-layouts  24.8 us (7%)
  blocking collectives  17.5 us (5%)
  between operations  14 us (4%)
  other arithmetic  11.9 us (4%)
  starting transfers between devices  4.93 us (1%)
    psum x1, waiting for transfers between devices, shards(): summed = lax.psum(term.astype(jnp.bfloat16), 'cb').astype(jnp.float32)  81.4 us
    all_gather x1, waiting for transfers between devices, shards(): lax.all_gather(input_weight, 'seq', axis=1, tiled=True)[0]  50.7 us
    all_to_all x1, waiting for transfers between devices, shards(): lax.all_to_all(packed, 'cb', split_axis=1, concat_axis=0, tiled=True)  37.5 us
    all_gather x1, waiting for transfers between devices, shards(): value_piece = lax.all_gather(projected[2], 'seq', axis=1, tiled=True)  24.7 us
    all_gather x1, waiting for transfers between devices, shards(): key_piece = lax.all_gather(projected[1], 'seq', axis=1, tiled=True)  21.2 us
    all_to_all x1, blocking collectives, shards(): lax.all_to_all(result, 'cb', split_axis=0, concat_axis=1, tiled=True)  17.5 us
    dot_general x3, matrix products, shards(): jnp.dot(normed, temporal_qkv[which], preferred_element_type=jnp.float32)  11.6 us
  transfers between devices with their start and end apart: 5, of which 5 were waited for; matrix products, arithmetic and copies ran while one was open for 7% of the time, Pallas kernels for 0%

commit v1 on v0

--- a/solution.py
+++ b/solution.py
@@ -69,7 +69,7 @@
         .reshape(row_count, head_cols)
     )
     term = jnp.dot(mixed, temporal_out, preferred_element_type=jnp.float32)
-    summed = lax.psum(term.astype(jnp.bfloat16), "cb").astype(jnp.float32)
+    summed = jnp.sum(lax.all_gather(term.astype(jnp.bfloat16), "cb"), axis=0).astype(jnp.float32)
     temporal = (hidden_f.reshape(row_count, width) + summed).astype(jnp.bfloat16)
     projected_in = jnp.dot(
         temporal,

time: 335 us -> 394 us (1.18)
  waiting for transfers between devices: 216 us -> 271 us
  other arithmetic: 11.9 us -> 19 us
    all_gather x0 -> x1, waiting for transfers between devices: none -> 145 us  [shards(): lax.all_gather(term.astype(jnp.bfloat16), 'cb')]
    psum x1 -> x0, waiting for transfers between devices: 81.4 us -> none  [shards(): summed = lax.psum(term.astype(jnp.bfloat16), 'cb').astype(jnp.float32)]
    all_gather x1, waiting for transfers between devices: 50.7 us -> 42.6 us  [shards(): lax.all_gather(input_weight, 'seq', axis=1, tiled=True)[0]]
    reduce_sum x0 -> x1, other arithmetic: none -> 6.89 us  [shards(): jnp.sum(lax.all_gather(term.astype(jnp.bfloat16), 'cb'), axis=0)]
where the time goes in v1:
time: 394 us
  waiting for transfers between devices  271 us (69%)
  matrix products  42.2 us (11%)
  local copies, waits for them, and re-layouts  24.8 us (6%)
  other arithmetic  19 us (5%)
  blocking collectives  17.5 us (4%)
  between operations  14.1 us (4%)
  starting transfers between devices  4.96 us (1%)
    all_gather x1, waiting for transfers between devices, shards(): lax.all_gather(term.astype(jnp.bfloat16), 'cb')  145 us
    all_gather x1, waiting for transfers between devices, shards(): lax.all_gather(input_weight, 'seq', axis=1, tiled=True)[0]  42.6 us
    all_to_all x1, waiting for transfers between devices, shards(): lax.all_to_all(packed, 'cb', split_axis=1, concat_axis=0, tiled=True)  37.5 us
    all_gather x1, waiting for transfers between devices, shards(): value_piece = lax.all_gather(projected[2], 'seq', axis=1, tiled=True)  24.7 us
    all_gather x1, waiting for transfers between devices, shards(): key_piece = lax.all_gather(projected[1], 'seq', axis=1, tiled=True)  21.2 us
    all_to_all x1, blocking collectives, shards(): lax.all_to_all(result, 'cb', split_axis=0, concat_axis=1, tiled=True)  17.5 us
    dot_general x3, matrix products, shards(): jnp.dot(normed, temporal_qkv[which], preferred_element_type=jnp.float32)  11.6 us
  transfers between devices with their start and end apart: 5, of which 5 were waited for; matrix products, arithmetic and copies ran while one was open for 7% of the time, Pallas kernels for 0%

profile of v1, /device:TPU:0, one launch (start us, length us, event | category | flops | bytes accessed | tf_op | source)
XLA Modules:
  0.0 393.7 jit_solution(14336444008673307403)
XLA Ops:
  7.2 0.0 copy-start
  7.2 0.0 all-gather.8.cloned.1.call-start
  7.2 2.2 fusion.2
  9.5 2.2 fusion.4
  11.7 0.0 copy-start.2
  11.7 1.3 copy-done.2
  13.0 3.5 fusion.66
  16.5 0.1 reshape.148
  16.6 0.7 copy.53
  17.3 0.0 all-gather.8.cloned.1.call-update
  17.3 0.0 all-gather.6.cloned.1.call-start
  17.4 4.1 %fusion.60 = bf16[256,512]{1,0:T(8,128)(2,1)S(1)} fusion(bf16[256,4096]{1,0:T(8,128)(2,1)} %bitcast.121, bf16[3,4096,512]{2,1,0:T(8,128)(2,1)} %param.12), kind=kOutput, calls=%fused_computation.55 | convolution fusion | flops 1073872896 | bytes 6553600 | tf_op jit(solution)/shard_map/dot_general | solution.py:37
  21.5 0.1 reshape.146
  21.5 0.9 copy.52
  22.4 0.0 all-gather.6.cloned.1.call-update
  22.4 0.0 all-gather.12.cloned.1.call-start
  22.5 4.1 %fusion.63 = bf16[256,512]{1,0:T(8,128)(2,1)S(1)} fusion(bf16[256,4096]{1,0:T(8,128)(2,1)} %bitcast.122, bf16[3,4096,512]{2,1,0:T(8,128)(2,1)} %param.12), kind=kOutput, calls=%fused_computation.56 | convolution fusion | flops 1073872896 | bytes 6553600 | tf_op jit(solution)/shard_map/dot_general | solution.py:37
  26.5 0.1 reshape.147
  26.6 0.1 iota_compare_fusion
  26.8 21.2 %all-gather.8.cloned.1.call-done = bf16[2,1024,4,128]{3,1,2,0:T(8,128)(2,1)} async-done(((bf16[2,128,4,128]{3,1,2,0:T(8,128)(2,1)}), bf16[2,1024,4,128]{3,1,2,0:T(8,128)(2,1)}) %all-gather.8.cloned.1.call-update) | async-done | bytes 2097168 | tf_op jit(solution)/shard_map/all_gather | solution.py:45
  48.0 2.6 fusion.15
  50.6 0.0 copy-start.1
  50.6 1.9 copy-done.1
  52.6 1.3 fusion.16
  53.9 24.7 %all-gather.6.cloned.1.call-done = bf16[2,1024,4,128]{1,3,2,0:T(8,128)(2,1)} async-done(((bf16[2,128,4,128]{1,3,2,0:T(8,128)(2,1)}), bf16[2,1024,4,128]{1,3,2,0:T(8,128)(2,1)}) %all-gather.6.cloned.1.call-update) | async-done | bytes 2097168 | tf_op jit(solution)/shard_map/all_gather | solution.py:46
  78.6 4.2 %fusion.76 = bf16[2,128,4,128]{1,3,2,0:T(8,128)(2,1)S(1)} fusion(bf16[2,1024,4,128]{1,3,2,0:T(8,128)(2,1)} %all-gather.6.cloned.1.call-done, f32[2,4,128,1024]{3,2,1,0:T(8,128)} %copy-done.1, f32[2,4,128]{2,1,0:T(4,128)S(1)} %broadcast_maximum_fusion, pred[128,1024]{1,0:T(8,128)(4,1)S(1)} %iota_compare_fusion, f32[2,128,4]{1,2,0:T(4,128)S(1)} %bitcast.127), kind=kOutput, calls=%fused_computation.66 | convolution fusion | flops 273940480 | bytes 6692864 | tf_op jit(solution)/shard_map/shqk,skhd->sqhd/dot_general | solution.py:58
  82.8 0.2 copy.55
  83.0 0.0 copy-start.3
  83.0 4.8 %convolution_convert_fusion = bf16[256,4096]{1,0:T(8,128)(2,1)} fusion(bf16[512,4096]{1,0:T(8,128)(2,1)} %param.13, bf16[32,8,4,128]{3,2,1,0:T(4,128)(2,1)S(1)} %bitcast.125), kind=kOutput, calls=%fused_computation.6 | convolution fusion | flops 1074790400 | bytes 6553600 | tf_op jit(solution)/shard_map/dot_general | solution.py:71
  87.8 0.0 all-gather.12.cloned.1.call-update
  87.8 0.2 all-gather.10.cloned.1.call-start
  88.0 0.3 all-gather.10.cloned.1.call-update
  88.4 0.0 copy-done.3
  88.4 4.3 %gather_fusion = bf16[256,1024]{1,0:T(8,128)(2,1)S(1)} fusion(bf16[2048,1024]{1,0:T(8,128)(2,1)} %bitcast.118, s32[1024]{0:T(1024)S(1)} %pad_clamp_fusion), kind=kCustom, calls=%fused_computation | custom fusion | bytes 1049600 | tf_op jit(solution)/shard_map/jit(_take)/gather | solution.py:79
  92.7 144.8 %all-gather.12.cloned.1.call-done = bf16[1024,4096]{1,0:T(8,128)(2,1)} async-done(((bf16[256,4096]{1,0:T(8,128)(2,1)}), bf16[1024,4096]{1,0:T(8,128)(2,1)}) %all-gather.12.cloned.1.call-update) | async-done | bytes 8388624 | tf_op jit(solution)/shard_map/all_gather | solution.py:72
  237.6 6.9 %reduce_sum.50 = bf16[256,4096]{1,0:T(8,128)(2,1)} reduce(bf16[4,256,4096]{2,1,0:T(8,128)(2,1)} %bitcast.115, bf16[]{:T(256)} %constant.39.clone.1), dimensions={0}, to_apply=%region_3.4 | reduce | flops 3145728 | bytes 10485762 | tf_op jit(solution)/shard_map/reduce_sum | solution.py:72
  244.4 4.7 %fusion.5 = bf16[2,128,4096]{2,1,0:T(8,128)(2,1)} fusion(bf16[2,128,4096]{2,1,0:T(8,128)(2,1)} %param.10, bf16[2,128,4096]{2,1,0:T(8,128)(2,1)} %bitcast.116), kind=kLoop, calls=%fused_computation.10 | loop fusion | flops 4194304 | bytes 6291456 | tf_op jit(solution)/shard_map/convert_element_type | solution.py:73
  249.1 42.6 %all-gather.10.cloned.1.call-done = bf16[1,4096,1024]{2,1,0:T(8,128)(2,1)} async-done(((bf16[1,512,1024]{2,1,0:T(8,128)(2,1)}), bf16[1,4096,1024]{2,1,0:T(8,128)(2,1)}) %all-gather.10.cloned.1.call-update) | async-done | bytes 8388624 | tf_op jit(solution)/shard_map/all_gather | solution.py:76
  291.8 6.6 %fusion.69 = (f32[256]{0:T(256)S(1)}, bf16[256,1024]{1,0:T(8,128)(2,1)S(1)}) fusion(bf16[256,1024]{1,0:T(8,128)(2,1)S(1)} %gather_fusion, pred[256]{0:T(512)(128)(4,1)S(1)} %compare_and_fusion, bf16[256,4096]{1,0:T(8,128)(2,1)} %bitcast.119, bf16[1,4096,1024]{2,1,0:T(8,128)(2,1)} %all-gather.10.cloned.1.call-done), kind=kOutput, calls=%fused_computation.58 | convolution fusion | flops 2149318400 | bytes 11535616 | tf_op jit(solution)/shard_map/dot_general | solution.py:74
  298.4 0.0 copy-start.5
  298.4 0.0 copy-done.4
  298.4 2.5 fusion.48
  301.0 0.0 slice-done
  301.0 0.0 slice-done.1
  301.0 0.8 fusion.51
  301.8 0.0 copy-done.5
  301.8 0.8 fusion.54
  302.5 1.2 pad_maximum_fusion
  303.8 4.6 %all-to-all-start = ((bf16[1,4,64,3072]{3,2,0,1:T(8,128)(2,1)}), bf16[1,4,64,3072]{3,2,0,1:T(8,128)(2,1)}, u32[]{:S(2)}, u32[]{:S(2)}) async-start(bf16[1,4,64,3072]{3,2,0,1:T(8,128)(2,1)} %bitcast.117), calls=%async_computation | async-start | bytes 3145728 | tf_op jit(solution)/shard_map/all_to_all | solution.py:97
  308.4 37.5 %all-to-all-done = bf16[1,4,64,3072]{3,2,0,1:T(8,128)(2,1)} async-done(((bf16[1,4,64,3072]{3,2,0,1:T(8,128)(2,1)}), bf16[1,4,64,3072]{3,2,0,1:T(8,128)(2,1)}, u32[]{:S(2)}, u32[]{:S(2)}) %all-to-all-start) | async-done | bytes 1572896 | tf_op jit(solution)/shard_map/all_to_all | solution.py:97
  345.9 4.9 %reshape.153 = bf16[4,64,3,16,64]{4,3,2,1,0:T(8,128)(2,1)} reshape(bf16[1,4,64,3072]{3,2,0,1:T(8,128)(2,1)} %all-to-all-done) | data formatting | bytes 3145728 | tf_op jit(solution)/shard_map/reshape | solution.py:99
  350.7 3.5 fusion.92
  354.2 2.9 fusion.72
  357.1 2.4 copy.60
  359.5 0.1 fusion.83
  359.6 0.1 fusion.84
  359.7 1.8 copy.61
  361.5 1.1 copy.62
  362.6 2.9 fusion.35
  365.5 0.1 copy.63
  365.6 1.5 reshape.154
  367.1 17.5 %all_to_all.8 = bf16[4,1,64,1024]{3,2,1,0:T(8,128)(2,1)S(1)} all-to-all(bf16[4,1,64,1024]{3,2,1,0:T(8,128)(2,1)} %bitcast.123), channel_id=1, replica_groups=mesh['seq'=8,'cb'=4] {'cb'}, dimensions={0} | all-to-all | bytes 1048576 | tf_op jit(solution)/shard_map/all_to_all | solution.py:123
  384.6 0.0 copy-done
  384.6 2.5 fusion.45
  (12 shorter events, 0.1 us)
Async XLA Ops:
  7.2 377.4 %copy-start = (bf16[1,1024,1024]{2,1,0:T(8,128)(2,1)S(1)}, bf16[1,1024,1024]{2,1,0:T(8,128)(2,1)}, u32[]{:S(2)}) copy-start(bf16[1,1024,1024]{2,1,0:T(8,128)(2,1)} %param.19) | copy-start | bytes 6291460
  7.2 40.8 %all-gather.8.cloned.1.call-start = ((), (), s32[]{:S(2)}) async-start(), calls=%async_computation.3 | async-start | bytes 2359296 | tf_op jit(solution)/shard_map/all_gather | solution.py:45
  11.7 1.3 copy-start.2
  17.3 61.2 %all-gather.6.cloned.1.call-start = ((), (), s32[]{:S(2)}) async-start(), calls=%async_computation.2 | async-start | bytes 2359296 | tf_op jit(solution)/shard_map/all_gather | solution.py:46
  22.4 215.1 %all-gather.12.cloned.1.call-start = ((), (), s32[]{:S(2)}) async-start(), calls=%async_computation.5 | async-start | bytes 10485760 | tf_op jit(solution)/shard_map/all_gather | solution.py:72
  50.6 1.9 copy-start.1
  83.0 5.4 %copy-start.3 = (s32[2,128,1]{1,2,0:T(1,128)S(1)}, s32[2,128,1]{1,2,0:T(1,128)}, u32[]{:S(2)}) copy-start(s32[2,128,1]{1,2,0:T(1,128)} %param.14) | copy-start | bytes 3076
  87.8 204.0 %all-gather.10.cloned.1.call-start = ((), (), s32[]{:S(2)}) async-start(), calls=%async_computation.4 | async-start | bytes 9437184 | tf_op jit(solution)/shard_map/all_gather | solution.py:76
  291.8 9.2 %slice-start = ((s8[6291456]{0:T(1024)(128)(4,1)}), s8[4194304]{0:T(1024)(128)(4,1)S(1)}, s32[]{:S(2)}) async-start(s8[6291456]{0:T(1024)(128)(4,1)} %bitcast.129), calls=%async_computation.6 | async-start | bytes 8388608
  291.8 6.6 %copy-start.4 = (f32[1,1024]{1,0:T(1,128)S(1)}, f32[1,1024]{1,0:T(1,128)}, u32[]{:S(2)}) copy-start(f32[1,1024]{1,0:T(1,128)} %param.17) | copy-start | bytes 12292
  291.8 9.2 %slice-start.1 = ((s8[6291456]{0:T(1024)(128)(4,1)}), s8[2097152]{0:T(1024)(128)(4,1)S(1)}, s32[]{:S(2)}) async-start(s8[6291456]{0:T(1024)(128)(4,1)} %bitcast.129), calls=%async_computation.7 | async-start | bytes 4194304
  298.4 3.4 copy-start.5
  303.8 42.1 %all-to-all-start = ((bf16[1,4,64,3072]{3,2,0,1:T(8,128)(2,1)}), bf16[1,4,64,3072]{3,2,0,1:T(8,128)(2,1)}, u32[]{:S(2)}, u32[]{:S(2)}) async-start(bf16[1,4,64,3072]{3,2,0,1:T(8,128)(2,1)} %bitcast.117), calls=%async_computation | async-start | bytes 3145728 | tf_op jit(solution)/shard_map/all_to_all | solution.py:97
Sparse Core Ops, SparseCore 0:
  17.5 30.4 all-gather.7
  50.4 28.0 all-gather.5
  87.9 149.5 all-gather.11
  239.3 52.4 all-gather.9
